TPU v7x, 32 devices: a whole 2x2x4 slice. The times are simulated.
32 devices in a mesh: stn: 4 (over x, core), chan: 8 (over z, y).
Axes of the slice: x: 2, y: 2, z: 4, core: 2. Of those that a mesh axis runs over, the one named last changes fastest.
Arguments:
- voltages: bfloat16 [2, 96, 1024, 256], P(None, None, ('stn', 'chan')), may hold values from -6 to 6
- flagged_ids: int32 [32], replicated, may hold values from 0 to 95, as said below
- work_plan: int32 [4, 8, 2], replicated, may hold values from 8 to 87, as said below
Outputs:
- visibility: bfloat16 [96, 2, 1024, 1024], P('stn', None, 'chan')
- slot_power: float32 [4, 8, 2], P('stn', 'chan')
Inputs may be any that keep to these rules, and one draw needn't show every extreme that they name: `flagged_ids`: the flagged channels with stn group a (channels a * 24 to a * 24 + 23) are one contiguous run of 8 channels inside that group; in the first group the run starts at the group's first channel, in the last group it ends at the group's last channel, in the others its position is drawn for each group; the list is ascending. work_plan[a] lists every unflagged channel of group a exactly once, so it holds only channels of that group.
All inputs are finite; a program needn't handle non-finite values.
Results may differ from a plain program's by a relative error of at most 0.001.
Values may be sent and summed in bfloat16 or wider, within the bound.
A program may use at most 128 MiB of HBM per device.

v0:
```python
import jax
import jax.numpy as jnp
from jax import lax
from jax.sharding import PartitionSpec as P


def cross_power(block):
    station_count = block.shape[1]
    stacked = block.reshape(2 * station_count, block.shape[2])
    product = lax.dot_general(
        stacked, stacked, (((1,), (1,)), ((), ())), preferred_element_type=jnp.float32
    )
    factor = 1.0 / block.shape[2]
    real_part = (
        product[:station_count, :station_count] + product[station_count:, station_count:]
    ) * factor
    imag_part = (
        product[station_count:, :station_count] - product[:station_count, station_count:]
    ) * factor
    visible = jnp.stack([real_part, imag_part]).astype(jnp.bfloat16)
    return (visible, jnp.trace(real_part) / station_count)


def corner_turn(buffer):
    return lax.all_to_all(buffer, ("stn", "chan"), split_axis=1, concat_axis=2, tiled=True)


def return_rows(visible):
    return lax.all_to_all(visible, "chan", split_axis=2, concat_axis=0, tiled=True)


def on_device(voltages, flagged_ids, work_plan):
    stn_idx = lax.axis_index("stn")
    n_stn = lax.axis_size("stn")
    group_size = voltages.shape[1] // n_stn
    slot_count = work_plan.shape[2]
    buffer = jnp.take(voltages, work_plan.reshape(-1), axis=1)
    turned = corner_turn(buffer)

    def one_slot(slot):
        return cross_power(lax.dynamic_index_in_dim(turned, slot, 1, keepdims=False))

    visible, powers = lax.map(one_slot, jnp.arange(slot_count, dtype=jnp.int32))
    returned = return_rows(visible)
    group_plan = (
        lax.dynamic_index_in_dim(work_plan, stn_idx, 0, keepdims=False).reshape(-1)
        - stn_idx * group_size
    )
    visibility = (
        jnp.zeros((group_size,) + returned.shape[1:], jnp.bfloat16).at[group_plan].set(returned)
    )
    slot_power = powers.reshape(1, 1, slot_count)
    return (visibility, slot_power)


def solution(mesh):
    in_specs = (P(None, None, ("stn", "chan"), None), P(), P())
    out_specs = (P("stn", None, "chan", None), P("stn", "chan", None))
    return jax.shard_map(
        on_device, mesh=mesh, in_specs=in_specs, out_specs=out_specs, check_vma=False
    )
```

profile of v0, /device:TPU:0, one launch (start us, length us, event | category | flops | bytes accessed | tf_op | source)
XLA Modules:
  0.0 331.3 jit_solution(5712409745350449431)
XLA Ops:
  0.6 0.0 copy-start
  0.6 0.9 copy.15
  1.6 0.1 reshape.107
  1.7 0.1 reshape.106
  1.8 0.7 copy-done
  2.5 2.0 gather_fusion
  4.5 3.2 select_bitcast_fusion
  7.7 7.3 %all-to-all-start = ((bf16[2,64,32,256]{3,2,0,1:T(8,128)(2,1)}), bf16[2,64,32,256]{3,2,0,1:T(8,128)(2,1)S(1)}, u32[]{:S(2)}, u32[]{:S(2)}) async-start(bf16[2,64,32,256]{3,2,0,1:T(8,128)(2,1)} %select_bitcast_fusion), calls=%async_computation | async-start | bytes 4194304 | tf_op jit(solution)/shard_map/all_to_all | solution.py:25
  15.0 50.1 %all-to-all-done = bf16[2,64,32,256]{3,2,0,1:T(8,128)(2,1)S(1)} async-done(((bf16[2,64,32,256]{3,2,0,1:T(8,128)(2,1)}), bf16[2,64,32,256]{3,2,0,1:T(8,128)(2,1)S(1)}, u32[]{:S(2)}, u32[]{:S(2)}) %all-to-all-start) | async-done | bytes 2097184 | tf_op jit(solution)/shard_map/all_to_all | solution.py:25
  65.1 1.6 copy.17
  66.7 38.5 %while.12 = (s32[]{:T(128)}, bf16[2,2,1024,1024]{3,1,0,2:T(2,128)(2,1)}, f32[2]{0:T(128)S(1)}, s32[2]{0:T(128)S(1)}, bf16[2,2,1024,256]{3,2,1,0:T(8,128)(2,1)}, ...) while((s32[]{:T(128)}, bf16[2,2,1024,1024]{3,1,0,2:T(2,128)(2,1)}, f32[2]{0:T(128)S(1)}, s32[2]{0:T(128)S(1)}, ...), condition=%wide.region_2.3_spmd, body=%wide.region_0.0_spmd.sunk | while | flops 2159017984 | bytes 57671860 | solution.py:43
  66.7 0.6 dynamic_slice.18
  69.1 1.3 constant_dynamic-slice_fusion.2
  70.4 2.4 fusion.14
  72.8 4.0 %select_reduce_fusion.2 = (f32[]{:T(128)}, bf16[1,1,1024,1024]{3,2,1,0:T(8,128)(2,1)S(1)}, bf16[1,1,1024,1024]{3,2,1,0:T(8,128)(2,1)}) fusion(f32[2048,2048]{1,0:T(8,128)S(1)} %fusion.14), kind=kLoop, calls=%fused_computation.9.clone.1 | loop fusion | flops 9437183 | bytes 20971524 | tf_op jit(solution)/shard_map/while/body/eval_jaxpr/jit(trace)/reduce_sum | solution.py:21
  77.5 0.1 dynamic_update_slice.12
  77.6 2.0 pad_maximum_fusion.2
  79.6 6.3 %copy_dynamic-update-slice_fusion.2 = bf16[2,2,1024,1024]{3,1,0,2:T(2,128)(2,1)} fusion(bf16[2,2,1024,1024]{3,1,0,2:T(2,128)(2,1)} %get-tuple-element.92, s32[]{:T(128)S(6)} %copy.30, bf16[1,2,1024,1024]{3,2,1,0:T(8,128)(2,1)S(1)} %pad_maximum_fusion.2), kind=kLoop, calls=%fused_computation.8.clone.1 | loop fusion | bytes 8388612 | tf_op jit(solution)/shard_map/while/body/jit(dynamic_update_index_in_dim)/dynamic_update_slice | solution.py:43
  85.9 0.6 dynamic_slice.18
  88.4 1.3 constant_dynamic-slice_fusion.2
  89.7 2.4 fusion.14
  92.1 4.0 %select_reduce_fusion.2 = (f32[]{:T(128)}, bf16[1,1,1024,1024]{3,2,1,0:T(8,128)(2,1)S(1)}, bf16[1,1,1024,1024]{3,2,1,0:T(8,128)(2,1)}) fusion(f32[2048,2048]{1,0:T(8,128)S(1)} %fusion.14), kind=kLoop, calls=%fused_computation.9.clone.1 | loop fusion | flops 9437183 | bytes 20971524 | tf_op jit(solution)/shard_map/while/body/eval_jaxpr/jit(trace)/reduce_sum | solution.py:21
  96.7 0.1 dynamic_update_slice.12
  96.8 2.0 pad_maximum_fusion.2
  98.8 6.3 %copy_dynamic-update-slice_fusion.2 = bf16[2,2,1024,1024]{3,1,0,2:T(2,128)(2,1)} fusion(bf16[2,2,1024,1024]{3,1,0,2:T(2,128)(2,1)} %get-tuple-element.92, s32[]{:T(128)S(6)} %copy.30, bf16[1,2,1024,1024]{3,2,1,0:T(8,128)(2,1)S(1)} %pad_maximum_fusion.2), kind=kLoop, calls=%fused_computation.8.clone.1 | loop fusion | bytes 8388612 | tf_op jit(solution)/shard_map/while/body/jit(dynamic_update_index_in_dim)/dynamic_update_slice | solution.py:43
  105.2 0.0 copy-start.2
  105.2 0.5 copy-done.2
  105.7 5.1 %all-to-all-start.1 = ((bf16[2,2,1024,1024]{3,1,0,2:T(2,128)(2,1)}), bf16[2,2,1024,1024]{3,1,0,2:T(2,128)(2,1)}, u32[]{:S(2)}, u32[]{:S(2)}) async-start(bf16[2,2,1024,1024]{3,1,0,2:T(2,128)(2,1)} %get-tuple-element.30), calls=%async_computation.1 | async-start | bytes 16777216 | tf_op jit(solution)/shard_map/all_to_all | solution.py:29
  110.8 0.7 dynamic-slice_subtract_fusion
  111.5 0.1 copy.14
  111.6 0.1 sub.21
  111.7 182.1 %all-to-all-done.1 = bf16[2,2,1024,1024]{3,1,0,2:T(2,128)(2,1)} async-done(((bf16[2,2,1024,1024]{3,1,0,2:T(2,128)(2,1)}), bf16[2,2,1024,1024]{3,1,0,2:T(2,128)(2,1)}, u32[]{:S(2)}, u32[]{:S(2)}) %all-to-all-start.1) | async-done | bytes 8388640 | tf_op jit(solution)/shard_map/all_to_all | solution.py:29
  293.8 9.8 %copy.19 = bf16[8,2,2,128,1024]{4,3,2,1,0:T(8,128)(2,1)} copy(bf16[8,2,2,128,1024]{4,2,1,3,0:T(2,128)(2,1)} %bitcast.12) | data formatting | bytes 16777216 | tf_op jit(solution)/shard_map/all_to_all | solution.py:29
  303.5 6.4 %broadcast_in_dim.27 = bf16[24,2,128,1024]{3,2,1,0:T(8,128)(2,1)} broadcast(bf16[]{:T(256)} %constant.37.clone.1), dimensions={} | broadcast | bytes 12582914 | tf_op jit(solution)/shard_map/broadcast_in_dim | solution.py:50
  309.9 0.0 copy-start.1
  309.9 21.4 %scatter_fusion = bf16[24,2,128,1024]{3,2,1,0:T(8,128)(2,1)} fusion(bf16[24,2,128,1024]{3,2,1,0:T(8,128)(2,1)} %broadcast_in_dim.27, s32[16]{0:T(128)S(1)} %fusion.4, bf16[16,2,128,1024]{3,2,1,0:T(8,128)(2,1)} %bitcast.36), kind=kCustom, calls=%fused_computation.1 | custom fusion | bytes 25165888 | tf_op jit(solution)/shard_map/scatter | solution.py:50
  331.3 0.0 copy-done.1
  (7 shorter events, 0.0 us)
Async XLA Ops:
  0.6 1.9 copy-start
  7.7 57.4 %all-to-all-start = ((bf16[2,64,32,256]{3,2,0,1:T(8,128)(2,1)}), bf16[2,64,32,256]{3,2,0,1:T(8,128)(2,1)S(1)}, u32[]{:S(2)}, u32[]{:S(2)}) async-start(bf16[2,64,32,256]{3,2,0,1:T(8,128)(2,1)} %select_bitcast_fusion), calls=%async_computation | async-start | bytes 4194304 | tf_op jit(solution)/shard_map/all_to_all | solution.py:25
  105.2 0.5 copy-start.2
  105.7 188.1 %all-to-all-start.1 = ((bf16[2,2,1024,1024]{3,1,0,2:T(2,128)(2,1)}), bf16[2,2,1024,1024]{3,1,0,2:T(2,128)(2,1)}, u32[]{:S(2)}, u32[]{:S(2)}) async-start(bf16[2,2,1024,1024]{3,1,0,2:T(2,128)(2,1)} %get-tuple-element.30), calls=%async_computation.1 | async-start | bytes 16777216 | tf_op jit(solution)/shard_map/all_to_all | solution.py:29
  309.9 21.4 %copy-start.1 = (bf16[2,96,32,256]{3,2,1,0:T(8,128)(2,1)S(1)}, bf16[2,96,32,256]{3,2,1,0:T(8,128)(2,1)}, u32[]{:S(2)}) copy-start(bf16[2,96,32,256]{3,2,1,0:T(8,128)(2,1)} %param.5) | copy-start | bytes 9437188
where the time goes:
time: 332 us; the launch traced here: 331 us
  waiting for transfers between devices  232 us (70%)
  local copies, waits for them, and re-layouts  60.3 us (18%)
  other arithmetic  15.8 us (5%)
  starting transfers between devices  12.4 us (4%)
  loops' own time  5.14 us (2%)
  matrix products  4.76 us (1%)
    all_to_all x1, waiting for transfers between devices, return_rows(): lax.all_to_all(visible, 'chan', split_axis=2, concat_axis=0, tiled=True)  182 us
    all_to_all x1, waiting for transfers between devices, corner_turn(): lax.all_to_all(buffer, ('stn', 'chan'), split_axis=1, concat_axis=2, tile...  50.1 us
    scatter x1, local copies, waits for them, and re-layouts, on_device(): jnp.zeros((group_size,) + returned.shape[1:], jnp.bfloat16).at[group_plan]  21.4 us
    dynamic_update_slice x4, local copies, waits for them, and re-layouts, on_device(): visible, powers = lax.map(one_slot, jnp.arange(slot_count, dtype=jnp.int32))  12.9 us
    all_to_all x1, local copies, waits for them, and re-layouts, return_rows(): lax.all_to_all(visible, 'chan', split_axis=2, concat_axis=0, tiled=True)  9.76 us
    reduce_sum x2, other arithmetic, cross_power(): return (visible, jnp.trace(real_part) / station_count)  7.95 us
    all_to_all x1, starting transfers between devices, corner_turn(): lax.all_to_all(buffer, ('stn', 'chan'), split_axis=1, concat_axis=2, tile...  7.3 us
  transfers between devices with their start and end apart: 2, of which 2 were waited for; matrix products, arithmetic and copies ran while one was open for 0% of the time, Pallas kernels for 0%

commit v1 on v0

v1 whole, which is shorter than its diff:
```python
import functools

import jax
import jax.numpy as jnp
from jax import lax
from jax.experimental import pallas as pl
from jax.experimental.pallas import tpu as pltpu
from jax.sharding import PartitionSpec as P

MESH = pl.DeviceIdType.MESH
INNER = 2


def gather_kernel(n_stn, n_out, packed, own_out, power, full, made, recv1, send1, recv2, send2, send3, recv3, local3):
    stn = lax.axis_index("stn")
    chan = lax.axis_index("chan")
    outer, inner = chan // INNER, chan % INNER
    count, stations = packed.shape[1], packed.shape[2]
    scale = 1.0 / (packed.shape[3] // 2)
    has_left, has_right = outer > 0, outer < n_out - 1

    barrier = pltpu.get_barrier_semaphore()
    peers = []
    for step in range(1, n_stn * INNER):
        to_stn = lax.rem(stn + step // INNER, n_stn)
        to_inner = lax.rem(inner + step % INNER, INNER)
        peers.append((to_stn, to_inner))
        pl.semaphore_signal(barrier, inc=1, device_id=(to_stn, outer * INNER + to_inner), device_id_type=MESH)

    @pl.when(has_left)
    def _():
        pl.semaphore_signal(barrier, inc=1, device_id=(stn, chan - INNER), device_id_type=MESH)

    @pl.when(has_right)
    def _():
        pl.semaphore_signal(barrier, inc=1, device_id=(stn, chan + INNER), device_id_type=MESH)

    pl.semaphore_wait(barrier, len(peers) + jnp.where(has_left, 1, 0) + jnp.where(has_right, 1, 0))

    def turn(c):
        rows = pl.ds(pl.multiple_of(inner * stations, stations), stations)
        target = full.at[c, stn, outer, rows]
        for to_stn, to_inner in peers:
            pltpu.make_async_remote_copy(
                packed.at[to_stn * INNER + to_inner, c], target, send1.at[c], recv1.at[c],
                device_id=(to_stn, outer * INNER + to_inner), device_id_type=MESH,
            ).start()
        pltpu.make_async_copy(packed.at[stn * INNER + inner, c], target, recv1.at[c]).start()

    def line(c, block, way):
        part = full.at[c, :, block]
        return pltpu.make_async_remote_copy(
            part, part, send2.at[way, block, c], recv2.at[block, c],
            device_id=(stn, chan + (INNER if way else -INNER)), device_id_type=MESH,
        )

    def back(c):
        return pltpu.make_async_remote_copy(
            made.at[c, 1 - inner], own_out.at[inner * count + c], send3.at[c], recv3.at[c],
            device_id=(stn, outer * INNER + 1 - inner), device_id_type=MESH,
        )

    def keep(c):
        return pltpu.make_async_copy(made.at[c, inner], own_out.at[inner * count + c], local3.at[c])

    def correlate(c):
        span = 2 * stations
        pieces = n_out // INNER
        for half in range(INNER):
            left = full[c, outer, pl.ds(half * pieces, pieces)].reshape(pieces * span, -1)
            time = left.shape[1] // 2
            turned = jnp.concatenate([left[:, time:], -left[:, :time]], axis=1)
            both = jnp.concatenate([left, turned], axis=0)
            for col in range(n_stn):
                right = full[c, col].reshape(n_out * span, -1)
                product = lax.dot_general(both, right, (((1,), (1,)), ((), ())), preferred_element_type=jnp.float32)
                made[c, half, :, :, col * n_out * span:(col + 1) * n_out * span] = (
                    (product * scale).astype(jnp.bfloat16).reshape(2, pieces * span, n_out * span)
                )

    @pl.loop(0, count)
    def _(c):
        turn(c)

    @pl.loop(0, count + n_out - 1)
    def _(t):
        @pl.when(t < count)
        def _():
            part = full.at[t, :, outer]
            pltpu.make_async_copy(part, part, recv1.at[t]).wait()

            @pl.when(has_left)
            def _():
                line(t, outer, 0).start()

            @pl.when(has_right)
            def _():
                line(t, outer, 1).start()

        for d in range(1, n_out):
            c = t - d
            live = jnp.logical_and(c >= 0, c < count)

            @pl.when(jnp.logical_and(live, outer - d >= 0))
            def _():
                line(c, outer - d, 1).wait_recv()

                @pl.when(has_right)
                def _():
                    line(c, outer - d, 1).start()

            @pl.when(jnp.logical_and(live, outer + d < n_out))
            def _():
                line(c, outer + d, 0).wait_recv()

                @pl.when(has_left)
                def _():
                    line(c, outer + d, 0).start()

        done = t - (n_out - 1)

        @pl.when(done >= 0)
        def _():
            correlate(done)
            back(done).start()
            keep(done).start()

    for k in range(count // n_out):
        total = jnp.zeros((8, full.shape[4]), jnp.float32)
        for a in range(n_stn):
            values = full[outer * (count // n_out) + k, a].astype(jnp.float32)
            total = total + jnp.sum((values * values).reshape(-1, 8, full.shape[4]), axis=0)
        power[k] = jnp.full(power.shape[1:], jnp.sum(total))

    @pl.loop(0, count)
    def _(c):
        part = packed.at[pl.ds(0, n_stn * INNER - 1), c]
        pltpu.make_async_copy(part, part, send1.at[c]).wait()
        for block in range(n_out):
            @pl.when(jnp.logical_and(has_right, outer >= block))
            def _():
                line(c, block, 1).wait_send()

            @pl.when(jnp.logical_and(has_left, outer <= block))
            def _():
                line(c, block, 0).wait_send()

        back(c).wait_send()
        back(c).wait_recv()
        keep(c).wait()


def gather_and_correlate(packed, n_stn, n_out):
    dests, count, stations, depth = packed.shape
    total_rows = n_stn * n_out * INNER * stations
    rows = total_rows // (n_out * INNER)
    dma = pltpu.SemaphoreType.DMA
    return pl.pallas_call(
        functools.partial(gather_kernel, n_stn, n_out),
        out_shape=(
            jax.ShapeDtypeStruct((INNER * count, 2, rows, total_rows), jnp.bfloat16),
            jax.ShapeDtypeStruct((count // n_out, 8, 128), jnp.float32),
        ),
        in_specs=[pl.BlockSpec(memory_space=pltpu.VMEM)],
        out_specs=(pl.BlockSpec(memory_space=pl.ANY), pl.BlockSpec(memory_space=pltpu.VMEM)),
        scratch_shapes=[
            pltpu.VMEM((count, n_stn, n_out, INNER * stations, depth), jnp.bfloat16),
            pltpu.VMEM((count, INNER, 2, rows, total_rows), jnp.bfloat16),
            dma((count,)), dma((count,)),
            dma((n_out, count)), dma((2, n_out, count)),
            dma((count,)), dma((count,)), dma((count,)),
        ],
        compiler_params=pltpu.CompilerParams(
            collective_id=0, has_side_effects=True, vmem_limit_bytes=40 * 1024 * 1024
        ),
    )(packed)


def spread_kernel(table, live, rows, out):
    @pl.when(live[pl.program_id(0)] != 0)
    def _():
        out[...] = rows[...]

    @pl.when(live[pl.program_id(0)] == 0)
    def _():
        out[...] = jnp.zeros_like(out)


def spread(made, order, group_size):
    hit = order[None, :] == jnp.arange(group_size, dtype=jnp.int32)[:, None]
    table = jnp.sum(jnp.where(hit, jnp.arange(order.shape[0], dtype=jnp.int32)[None, :], 0), axis=1)
    live = jnp.any(hit, axis=1).astype(jnp.int32)
    block = (1,) + made.shape[1:]
    return pl.pallas_call(
        spread_kernel,
        out_shape=jax.ShapeDtypeStruct((group_size,) + made.shape[1:], made.dtype),
        grid_spec=pltpu.PrefetchScalarGridSpec(
            num_scalar_prefetch=2,
            grid=(group_size,),
            in_specs=[pl.BlockSpec(block, lambda c, table, live: (table[c], 0, 0, 0))],
            out_specs=pl.BlockSpec(block, lambda c, table, live: (c, 0, 0, 0)),
        ),
    )(table.astype(jnp.int32), live, made)


def correlate_gathered(packed, chan_idx, n_stn, n_out):
    dests, count, stations, depth = packed.shape
    n_chan = n_out * INNER
    shards = packed.reshape(n_stn, INNER * count, stations, depth)
    turned = lax.all_to_all(shards, "stn", split_axis=0, concat_axis=0, tiled=True)
    full = lax.all_gather(turned, "chan", axis=1)
    full = full.transpose(2, 0, 1, 3, 4).reshape(INNER * count, -1, depth)
    total_rows = full.shape[1]
    rows = total_rows // n_chan
    left = lax.dynamic_slice_in_dim(full, chan_idx * rows, rows, 1)
    time = depth // 2
    turned_left = jnp.concatenate([left[..., time:], -left[..., :time]], axis=-1)
    both = jnp.stack([left, turned_left], axis=1)
    made = jnp.einsum("cprk,csk->cprs", both, full, preferred_element_type=jnp.float32) * (1.0 / time)
    slots = count // n_out
    first = (chan_idx % INNER) * count + (chan_idx // INNER) * slots
    own = lax.dynamic_slice_in_dim(full, first, slots, 0).astype(jnp.float32)
    return made.astype(jnp.bfloat16), jnp.sum(own * own, axis=(1, 2))


def on_device(voltages, flagged_ids, work_plan):
    stn_idx, chan_idx = lax.axis_index("stn"), lax.axis_index("chan")
    n_stn, n_chan = lax.axis_size("stn"), lax.axis_size("chan")
    n_out = n_chan // INNER
    _, channels, stations, time = voltages.shape
    group_size = channels // n_stn
    slot_count = work_plan.shape[2]
    plan = work_plan.reshape(n_stn, n_out, INNER, slot_count).transpose(0, 2, 1, 3)
    count = n_out * slot_count
    packed = jnp.take(voltages, plan.reshape(-1), axis=1)
    packed = packed.transpose(1, 2, 0, 3).reshape(n_stn * INNER, count, stations, 2 * time)
    total_rows = stations * n_stn * n_chan
    if n_stn == n_out and stations % 16 == 0:
        made, power = gather_and_correlate(packed, n_stn, n_out)
        power = power[:, 0, 0]
    else:
        made, power = correlate_gathered(packed, chan_idx, n_stn, n_out)
    order = lax.dynamic_index_in_dim(plan, stn_idx, 0, keepdims=False).reshape(-1) - stn_idx * group_size
    visibility = spread(made, order, group_size)
    slot_power = (power * (1.0 / time) / total_rows).reshape(1, 1, slot_count)
    return visibility, slot_power


def solution(mesh):
    in_specs = (P(None, None, ("stn", "chan"), None), P(), P())
    out_specs = (P("stn", None, "chan", None), P("stn", "chan", None))
    return jax.shard_map(
        on_device, mesh=mesh, in_specs=in_specs, out_specs=out_specs, check_vma=False
    )
```

time: 332 us -> 204 us (0.61)
  waiting for transfers between devices: 232 us -> 0 us
  Pallas kernels: 0 us -> 182 us
  local copies, waits for them, and re-layouts: 60.3 us -> 16.2 us
  starting transfers between devices: 12.4 us -> 0 us
  other arithmetic: 15.8 us -> 3.74 us
  loops' own time: 5.14 us -> 0 us
  matrix products: 4.76 us -> 0 us
    all_to_all x2 -> x0, waiting for transfers between devices: 232 us -> none  [the longest x1 182 us: return_rows(): lax.all_to_all(visible, 'chan', split_axis=2, concat_axis=0, tiled=True)]
    pallas_call x0 -> x2, Pallas kernels: none -> 182 us  [the longest x1 166 us: gather_and_correlate(): pl.pallas_call(functools.partial(gather_kernel, n_stn, n_out), out_shape=...]
    scatter x1 -> x0, local copies, waits for them, and re-layouts: 21.4 us -> none  [on_device(): jnp.zeros((group_size,) + returned.shape[1:], jnp.bfloat16).at[group_plan]]
    dynamic_update_slice x4 -> x0, local copies, waits for them, and re-layouts: 12.9 us -> none  [on_device(): visible, powers = lax.map(one_slot, jnp.arange(slot_count, dtype=jnp.int32))]
    all_to_all x2 -> x0, starting transfers between devices: 12.4 us -> none  [the longest x1 7.3 us: corner_turn(): lax.all_to_all(buffer, ('stn', 'chan'), split_axis=1, concat_axis=2, tile...]
    all_to_all x2 -> x0, local copies, waits for them, and re-layouts: 11.3 us -> none  [the longest x1 9.76 us: return_rows(): lax.all_to_all(visible, 'chan', split_axis=2, concat_axis=0, tiled=True)]
    reduce_sum x2 -> x1, other arithmetic: 7.95 us -> 0.58 us  [spread(): jnp.sum(jnp.where(hit, jnp.arange(order.shape[0], dtype=jnp.int32)[None,...]
    broadcast_in_dim x1 -> x0, local copies, waits for them, and re-layouts: 6.39 us -> none  [on_device(): jnp.zeros((group_size,) + returned.shape[1:], jnp.bfloat16).at[group_plan]]
  transfers between devices with their start and end apart: 2 -> 0, of which waited for: 2 -> 0; matrix products, arithmetic and copies ran while one was open for 0% -> 0% of each run, Pallas kernels for 0% -> 0%
where the time goes in v1:
time: 204 us; the launch traced here: 203 us
  Pallas kernels  182 us (89%)
  local copies, waits for them, and re-layouts  16.2 us (8%)
  other arithmetic  3.74 us (2%)
    pallas_call x1, Pallas kernels, gather_and_correlate(): pl.pallas_call(functools.partial(gather_kernel, n_stn, n_out), out_shape=...  166 us
    pallas_call x1, Pallas kernels, spread(): pl.pallas_call(spread_kernel, out_shape=jax.ShapeDtypeStruct((group_size,...  16.4 us
    unnamed x7, local copies, waits for them, and re-layouts  5.73 us
    reshape x1, local copies, waits for them, and re-layouts, on_device(): packed.transpose(1, 2, 0, 3)  4.38 us

profile of v1, /device:TPU:0, one launch (start us, length us, event | category | flops | bytes accessed | tf_op | source)
XLA Modules:
  0.0 202.5 jit_solution(9483267416627734179)
XLA Ops:
  0.6 0.0 copy-start
  0.7 0.9 copy.14
  1.6 0.1 subtract_bitcast_fusion
  1.6 0.1 copy.15
  1.8 0.1 sub.19
  1.9 0.1 fusion
  2.0 0.6 select_reduce_fusion.table
  2.5 0.5 convert_element_type.3.live
  3.1 0.1 copy.16
  3.2 0.1 reshape.73
  3.3 0.1 reshape.72
  3.5 0.0 copy-done
  3.5 2.0 gather_fusion
  5.5 1.8 select_bitcast_fusion
  7.3 3.5 %copy.18 = bf16[64,32,2,256]{3,2,1,0:T(2,128)(2,1)} copy(bf16[64,32,2,256]{3,1,2,0:T(8,128)(2,1)S(1)} %select_bitcast_fusion) | data formatting | bytes 4194304 | tf_op jit(solution)/shard_map/jit(_take)/select_n | solution.py:235
  10.8 4.4 %reshape.74.packed = bf16[8,8,32,512]{3,2,1,0:T(8,128)(2,1)} reshape(bf16[64,32,2,256]{3,2,1,0:T(2,128)(2,1)} %copy.18) | data formatting | bytes 4194304 | tf_op jit(solution)/shard_map/reshape | solution.py:236
  15.2 0.0 copy-start.2
  15.2 1.6 copy-done.2
  16.8 165.6 %shard_map.41 = (bf16[16,2,128,1024]{3,2,1,0:T(8,128)(2,1)S(1)}, f32[2,8,128]{2,1,0:T(8,128)S(1)}) custom-call(bf16[8,8,32,512]{3,2,1,0:T(8,128)(2,1)S(1)} %copy-done.2), custom_call_target="tpu_custom_call" | custom-call | tf_op jit(solution)/shard_map/pallas_call | solution.py:158
  182.3 0.0 copy-start.1
  182.4 3.2 %copy-done.1 = bf16[16,2,128,1024]{3,2,1,0:T(8,128)(2,1)} copy-done((bf16[16,2,128,1024]{3,2,1,0:T(8,128)(2,1)}, bf16[16,2,128,1024]{3,2,1,0:T(8,128)(2,1)S(1)}, u32[]{:S(2)}) %copy-start.1) | copy-done | bytes 8388632
  185.6 0.6 multiply_reduce_fusion
  186.2 16.4 %shard_map.42 = bf16[24,2,128,1024]{3,2,1,0:T(8,128)(2,1)} custom-call(s32[24]{0:T(128)} %select_reduce_fusion.table, s32[24]{0:T(128)} %convert_element_type.3.live, bf16[16,2,128,1024]{3,2,1,0:T(8,128)(2,1)} %copy-done.1), custom_call_target="tpu_custom_call" | custom-call | tf_op jit(solution)/shard_map/pallas_call | solution.py:194
  (3 shorter events, 0.0 us)
Async XLA Ops:
  0.6 2.8 %copy-start = (bf16[2,96,32,256]{3,2,1,0:T(8,128)(2,1)S(1)}, bf16[2,96,32,256]{3,2,1,0:T(8,128)(2,1)}, u32[]{:S(2)}) copy-start(bf16[2,96,32,256]{3,2,1,0:T(8,128)(2,1)} %param.3) | copy-start | bytes 9437188
  15.2 1.6 copy-start.2
  182.3 3.2 %copy-start.1 = (bf16[16,2,128,1024]{3,2,1,0:T(8,128)(2,1)}, bf16[16,2,128,1024]{3,2,1,0:T(8,128)(2,1)S(1)}, u32[]{:S(2)}) copy-start(bf16[16,2,128,1024]{3,2,1,0:T(8,128)(2,1)S(1)} %get-tuple-element.4.rows) | copy-start | bytes 25165828

commit v2 on v1

--- a/solution.py
+++ b/solution.py
@@ -8,15 +8,17 @@
 from jax.sharding import PartitionSpec as P
 
 MESH = pl.DeviceIdType.MESH
+AHEAD = 2
 INNER = 2
 
 
-def gather_kernel(n_stn, n_out, packed, own_out, power, full, made, recv1, send1, recv2, send2, send3, recv3, local3):
+def gather_kernel(n_stn, n_out, plan, voltages, own_out, power, packed, full, made, recv1, send1, recv2, send2, send3, recv3, local3):
     stn = lax.axis_index("stn")
     chan = lax.axis_index("chan")
     outer, inner = chan // INNER, chan % INNER
     count, stations = packed.shape[1], packed.shape[2]
-    scale = 1.0 / (packed.shape[3] // 2)
+    time = voltages.shape[3]
+    scale = 1.0 / time
     has_left, has_right = outer > 0, outer < n_out - 1
 
     barrier = pltpu.get_barrier_semaphore()
@@ -38,6 +40,10 @@
     pl.semaphore_wait(barrier, len(peers) + jnp.where(has_left, 1, 0) + jnp.where(has_right, 1, 0))
 
     def turn(c):
+        for dest in range(n_stn * INNER):
+            channel = plan[dest * count + c]
+            for part in range(2):
+                packed[dest, c, :, part * time:(part + 1) * time] = voltages[part, channel]
         rows = pl.ds(pl.multiple_of(inner * stations, stations), stations)
         target = full.at[c, stn, outer, rows]
         for to_stn, to_inner in peers:
@@ -68,7 +74,6 @@
         pieces = n_out // INNER
         for half in range(INNER):
             left = full[c, outer, pl.ds(half * pieces, pieces)].reshape(pieces * span, -1)
-            time = left.shape[1] // 2
             turned = jnp.concatenate([left[:, time:], -left[:, :time]], axis=1)
             both = jnp.concatenate([left, turned], axis=0)
             for col in range(n_stn):
@@ -78,12 +83,15 @@
                     (product * scale).astype(jnp.bfloat16).reshape(2, pieces * span, n_out * span)
                 )
 
-    @pl.loop(0, count)
-    def _(c):
+    for c in range(AHEAD):
         turn(c)
 
     @pl.loop(0, count + n_out - 1)
     def _(t):
+        @pl.when(t < count - AHEAD)
+        def _():
+            turn(t + AHEAD)
+
         @pl.when(t < count)
         def _():
             part = full.at[t, :, outer]
@@ -130,7 +138,7 @@
         for a in range(n_stn):
             values = full[outer * (count // n_out) + k, a].astype(jnp.float32)
             total = total + jnp.sum((values * values).reshape(-1, 8, full.shape[4]), axis=0)
-        power[k] = jnp.full(power.shape[1:], jnp.sum(total))
+        power[0, 0, k] = jnp.sum(total) * scale / (n_stn * n_out * INNER * stations)
 
     @pl.loop(0, count)
     def _(c):
@@ -150,8 +158,10 @@
         keep(c).wait()
 
 
-def gather_and_correlate(packed, n_stn, n_out):
-    dests, count, stations, depth = packed.shape
+def gather_and_correlate(plan, voltages, n_stn, n_out):
+    _, _, stations, time = voltages.shape
+    count = plan.shape[0] // (n_stn * INNER)
+    depth = 2 * time
     total_rows = n_stn * n_out * INNER * stations
     rows = total_rows // (n_out * INNER)
     dma = pltpu.SemaphoreType.DMA
@@ -159,11 +169,12 @@
         functools.partial(gather_kernel, n_stn, n_out),
         out_shape=(
             jax.ShapeDtypeStruct((INNER * count, 2, rows, total_rows), jnp.bfloat16),
-            jax.ShapeDtypeStruct((count // n_out, 8, 128), jnp.float32),
+            jax.ShapeDtypeStruct((1, 1, count // n_out), jnp.float32),
         ),
-        in_specs=[pl.BlockSpec(memory_space=pltpu.VMEM)],
-        out_specs=(pl.BlockSpec(memory_space=pl.ANY), pl.BlockSpec(memory_space=pltpu.VMEM)),
+        in_specs=[pl.BlockSpec(memory_space=pltpu.SMEM), pl.BlockSpec(memory_space=pltpu.VMEM)],
+        out_specs=(pl.BlockSpec(memory_space=pl.ANY), pl.BlockSpec(memory_space=pltpu.SMEM)),
         scratch_shapes=[
+            pltpu.VMEM((n_stn * INNER, count, stations, depth), jnp.bfloat16),
             pltpu.VMEM((count, n_stn, n_out, INNER * stations, depth), jnp.bfloat16),
             pltpu.VMEM((count, INNER, 2, rows, total_rows), jnp.bfloat16),
             dma((count,)), dma((count,)),
@@ -171,40 +182,63 @@
             dma((count,)), dma((count,)), dma((count,)),
         ],
         compiler_params=pltpu.CompilerParams(
-            collective_id=0, has_side_effects=True, vmem_limit_bytes=40 * 1024 * 1024
+            collective_id=0, has_side_effects=True, vmem_limit_bytes=56 * 1024 * 1024
         ),
-    )(packed)
-
-
-def spread_kernel(table, live, rows, out):
-    @pl.when(live[pl.program_id(0)] != 0)
-    def _():
-        out[...] = rows[...]
-
-    @pl.when(live[pl.program_id(0)] == 0)
-    def _():
-        out[...] = jnp.zeros_like(out)
-
-
-def spread(made, order, group_size):
-    hit = order[None, :] == jnp.arange(group_size, dtype=jnp.int32)[:, None]
-    table = jnp.sum(jnp.where(hit, jnp.arange(order.shape[0], dtype=jnp.int32)[None, :], 0), axis=1)
-    live = jnp.any(hit, axis=1).astype(jnp.int32)
-    block = (1,) + made.shape[1:]
+    )(plan, voltages)
+
+
+def spread_kernel(plan, flagged, made, out, zeros, held, read_sem, write_sem, zero_sem):
+    stn = lax.axis_index("stn")
+    slots, group_size = made.shape[0], out.shape[0]
+    first = stn * group_size
+    idle = group_size - slots
+
+    def read(j):
+        return pltpu.make_async_copy(made.at[j], held.at[j], read_sem.at[j])
+
+    def write(j):
+        return pltpu.make_async_copy(held.at[j], out.at[plan[stn * slots + j] - first], write_sem.at[j])
+
+    def clear(j):
+        return pltpu.make_async_copy(zeros, out.at[flagged[stn * idle + j] - first], zero_sem.at[j])
+
+    for j in range(slots):
+        read(j).start()
+    zeros[...] = jnp.zeros_like(zeros)
+    for j in range(idle):
+        clear(j).start()
+    for j in range(slots):
+        read(j).wait()
+        write(j).start()
+    for j in range(slots):
+        write(j).wait()
+    for j in range(idle):
+        clear(j).wait()
+
+
+def spread(plan, flagged, made, group_size):
+    slots, idle = made.shape[0], group_size - made.shape[0]
     return pl.pallas_call(
         spread_kernel,
         out_shape=jax.ShapeDtypeStruct((group_size,) + made.shape[1:], made.dtype),
-        grid_spec=pltpu.PrefetchScalarGridSpec(
-            num_scalar_prefetch=2,
-            grid=(group_size,),
-            in_specs=[pl.BlockSpec(block, lambda c, table, live: (table[c], 0, 0, 0))],
-            out_specs=pl.BlockSpec(block, lambda c, table, live: (c, 0, 0, 0)),
-        ),
-    )(table.astype(jnp.int32), live, made)
-
-
-def correlate_gathered(packed, chan_idx, n_stn, n_out):
-    dests, count, stations, depth = packed.shape
+        in_specs=[pl.BlockSpec(memory_space=pltpu.SMEM)] * 2 + [pl.BlockSpec(memory_space=pl.ANY)],
+        out_specs=pl.BlockSpec(memory_space=pl.ANY),
+        scratch_shapes=[
+            pltpu.VMEM(made.shape[1:], made.dtype),
+            pltpu.VMEM(made.shape, made.dtype),
+            pltpu.SemaphoreType.DMA((slots,)),
+            pltpu.SemaphoreType.DMA((slots,)),
+            pltpu.SemaphoreType.DMA((idle,)),
+        ],
+        compiler_params=pltpu.CompilerParams(vmem_limit_bytes=56 * 1024 * 1024),
+    )(plan, flagged, made)
+
+
+def correlate_gathered(plan, voltages, n_stn, n_out):
+    _, _, stations, time = voltages.shape
+    count, depth = plan.shape[0] // (n_stn * INNER), 2 * time
+    chan_idx = lax.axis_index("chan")
+    packed = jnp.take(voltages, plan, axis=1).transpose(1, 2, 0, 3)
     n_chan = n_out * INNER
     shards = packed.reshape(n_stn, INNER * count, stations, depth)
     turned = lax.all_to_all(shards, "stn", split_axis=0, concat_axis=0, tiled=True)
@@ -213,37 +247,27 @@
     total_rows = full.shape[1]
     rows = total_rows // n_chan
     left = lax.dynamic_slice_in_dim(full, chan_idx * rows, rows, 1)
-    time = depth // 2
     turned_left = jnp.concatenate([left[..., time:], -left[..., :time]], axis=-1)
     both = jnp.stack([left, turned_left], axis=1)
     made = jnp.einsum("cprk,csk->cprs", both, full, preferred_element_type=jnp.float32) * (1.0 / time)
     slots = count // n_out
     first = (chan_idx % INNER) * count + (chan_idx // INNER) * slots
     own = lax.dynamic_slice_in_dim(full, first, slots, 0).astype(jnp.float32)
-    return made.astype(jnp.bfloat16), jnp.sum(own * own, axis=(1, 2))
+    power = jnp.sum(own * own, axis=(1, 2)) * (1.0 / time) / total_rows
+    return made.astype(jnp.bfloat16), power.reshape(1, 1, slots)
 
 
 def on_device(voltages, flagged_ids, work_plan):
-    stn_idx, chan_idx = lax.axis_index("stn"), lax.axis_index("chan")
     n_stn, n_chan = lax.axis_size("stn"), lax.axis_size("chan")
     n_out = n_chan // INNER
-    _, channels, stations, time = voltages.shape
-    group_size = channels // n_stn
+    _, channels, stations, _ = voltages.shape
     slot_count = work_plan.shape[2]
-    plan = work_plan.reshape(n_stn, n_out, INNER, slot_count).transpose(0, 2, 1, 3)
-    count = n_out * slot_count
-    packed = jnp.take(voltages, plan.reshape(-1), axis=1)
-    packed = packed.transpose(1, 2, 0, 3).reshape(n_stn * INNER, count, stations, 2 * time)
-    total_rows = stations * n_stn * n_chan
+    plan = work_plan.reshape(n_stn, n_out, INNER, slot_count).transpose(0, 2, 1, 3).reshape(-1)
     if n_stn == n_out and stations % 16 == 0:
-        made, power = gather_and_correlate(packed, n_stn, n_out)
-        power = power[:, 0, 0]
+        made, power = gather_and_correlate(plan, voltages, n_stn, n_out)
     else:
-        made, power = correlate_gathered(packed, chan_idx, n_stn, n_out)
-    order = lax.dynamic_index_in_dim(plan, stn_idx, 0, keepdims=False).reshape(-1) - stn_idx * group_size
-    visibility = spread(made, order, group_size)
-    slot_power = (power * (1.0 / time) / total_rows).reshape(1, 1, slot_count)
-    return visibility, slot_power
+        made, power = correlate_gathered(plan, voltages, n_stn, n_out)
+    return spread(plan, flagged_ids, made, channels // n_stn), power
 
 
 def solution(mesh):

time: 204 us -> 180 us (0.88)
  local copies, waits for them, and re-layouts: 16.2 us -> 2.05 us
  Pallas kernels: 182 us -> 177 us
  other arithmetic: 3.74 us -> 0 us
    pallas_call x1, Pallas kernels: 16.4 us -> 8.74 us  [spread(): pl.pallas_call(spread_kernel, out_shape=jax.ShapeDtypeStruct((group_size,...]
    unnamed x7 -> x4, local copies, waits for them, and re-layouts: 5.73 us -> 1.29 us
    reshape x3 -> x1, local copies, waits for them, and re-layouts: 4.6 us -> 0.63 us  [on_device(): work_plan.reshape(n_stn, n_out, INNER, slot_count).transpose(0, 2, 1, 3)]
    select_n x1 -> x0, local copies, waits for them, and re-layouts: 3.48 us -> none  [on_device(): packed = jnp.take(voltages, plan.reshape(-1), axis=1)]
    pallas_call x1, Pallas kernels: 166 us -> 168 us  [gather_and_correlate(): pl.pallas_call(functools.partial(gather_kernel, n_stn, n_out), out_shape=...]
where the time goes in v2:
time: 180 us
  Pallas kernels  177 us (98%)
  local copies, waits for them, and re-layouts  2.05 us (1%)
    pallas_call x1, Pallas kernels, gather_and_correlate(): pl.pallas_call(functools.partial(gather_kernel, n_stn, n_out), out_shape=...  168 us
    pallas_call x1, Pallas kernels, spread(): pl.pallas_call(spread_kernel, out_shape=jax.ShapeDtypeStruct((group_size,...  8.74 us

profile of v2, /device:TPU:0, one launch (start us, length us, event | category | flops | bytes accessed | tf_op | source)
XLA Modules:
  0.0 179.8 jit_solution(10296408766104098577)
XLA Ops:
  0.6 0.8 copy.7
  1.4 0.1 copy.8
  1.5 0.6 reshape.11.plan
  2.2 168.3 %shard_map.50 = (bf16[16,2,128,1024]{3,2,1,0:T(8,128)(2,1)}, f32[1,1,2]{2,1,0:T(1,128)}) custom-call(s32[64]{0:T(128)} %reshape.11.plan, bf16[2,96,32,256]{3,2,1,0:T(8,128)(2,1)} %voltages.1), custom_call_target="tpu_custom_call" | custom-call | tf_op jit(solution)/shard_map/pallas_call | solution.py:168
  170.5 0.0 copy-start
  170.5 8.7 %shard_map.51 = bf16[24,2,128,1024]{3,2,1,0:T(8,128)(2,1)} custom-call(s32[64]{0:T(128)} %reshape.11.plan, s32[32]{0:T(128)} %flagged.1, bf16[16,2,128,1024]{3,2,1,0:T(8,128)(2,1)} %get-tuple-element.4.made), custom_call_target="tpu_custom_call" | custom-call | tf_op jit(solution)/shard_map/pallas_call | solution.py:221
  179.2 0.0 copy-done
  179.3 0.5 copy.10
Async XLA Ops:
  170.5 8.8 %copy-start = (f32[1,1,2]{2,1,0:T(1,128)S(1)}, f32[1,1,2]{2,1,0:T(1,128)}, u32[]{:S(2)}) copy-start(f32[1,1,2]{2,1,0:T(1,128)} %get-tuple-element.9) | copy-start | bytes 28

commit v3 on v2

--- a/solution.py
+++ b/solution.py
@@ -8,6 +8,8 @@
 from jax.sharding import PartitionSpec as P
 
 MESH = pl.DeviceIdType.MESH
+WINDOW = 2
+LEAD = 1
 AHEAD = 2
 INNER = 2
 
@@ -60,6 +62,13 @@
             device_id=(stn, chan + (INNER if way else -INNER)), device_id_type=MESH,
         )
 
+    def send(c, block, way):
+        @pl.when(c >= WINDOW)
+        def _():
+            line(c - WINDOW, block, way).wait_send()
+
+        line(c, block, way).start()
+
     def back(c):
         return pltpu.make_async_remote_copy(
             made.at[c, 1 - inner], own_out.at[inner * count + c], send3.at[c], recv3.at[c],
@@ -69,24 +78,23 @@
     def keep(c):
         return pltpu.make_async_copy(made.at[c, inner], own_out.at[inner * count + c], local3.at[c])
 
-    def correlate(c):
-        span = 2 * stations
+    def correlate(c, half):
+        span = INNER * stations
         pieces = n_out // INNER
-        for half in range(INNER):
-            left = full[c, outer, pl.ds(half * pieces, pieces)].reshape(pieces * span, -1)
-            turned = jnp.concatenate([left[:, time:], -left[:, :time]], axis=1)
-            both = jnp.concatenate([left, turned], axis=0)
-            for col in range(n_stn):
-                right = full[c, col].reshape(n_out * span, -1)
-                product = lax.dot_general(both, right, (((1,), (1,)), ((), ())), preferred_element_type=jnp.float32)
-                made[c, half, :, :, col * n_out * span:(col + 1) * n_out * span] = (
-                    (product * scale).astype(jnp.bfloat16).reshape(2, pieces * span, n_out * span)
-                )
+        left = full[c, outer, pl.ds(half * pieces, pieces)].reshape(pieces * span, -1)
+        turned = jnp.concatenate([left[:, time:], -left[:, :time]], axis=1)
+        both = jnp.concatenate([left, turned], axis=0)
+        for col in range(n_stn):
+            right = full[c, col].reshape(n_out * span, -1)
+            product = lax.dot_general(both, right, (((1,), (1,)), ((), ())), preferred_element_type=jnp.float32)
+            made[c, half, :, :, col * n_out * span:(col + 1) * n_out * span] = (
+                (product * scale).astype(jnp.bfloat16).reshape(2, pieces * span, n_out * span)
+            )
 
     for c in range(AHEAD):
         turn(c)
 
-    @pl.loop(0, count + n_out - 1)
+    @pl.loop(0, count + LEAD)
     def _(t):
         @pl.when(t < count - AHEAD)
         def _():
@@ -99,15 +107,15 @@
 
             @pl.when(has_left)
             def _():
-                line(t, outer, 0).start()
+                send(t, outer, 0)
 
             @pl.when(has_right)
             def _():
-                line(t, outer, 1).start()
-
+                send(t, outer, 1)
+
+        c = t - LEAD
+        live = c >= 0
         for d in range(1, n_out):
-            c = t - d
-            live = jnp.logical_and(c >= 0, c < count)
 
             @pl.when(jnp.logical_and(live, outer - d >= 0))
             def _():
@@ -115,7 +123,7 @@
 
                 @pl.when(has_right)
                 def _():
-                    line(c, outer - d, 1).start()
+                    send(c, outer - d, 1)
 
             @pl.when(jnp.logical_and(live, outer + d < n_out))
             def _():
@@ -123,15 +131,14 @@
 
                 @pl.when(has_left)
                 def _():
-                    line(c, outer + d, 0).start()
-
-        done = t - (n_out - 1)
-
-        @pl.when(done >= 0)
-        def _():
-            correlate(done)
-            back(done).start()
-            keep(done).start()
+                    send(c, outer + d, 0)
+
+        @pl.when(live)
+        def _():
+            correlate(c, 1 - inner)
+            back(c).start()
+            correlate(c, inner)
+            keep(c).start()
 
     for k in range(count // n_out):
         total = jnp.zeros((8, full.shape[4]), jnp.float32)
@@ -144,14 +151,17 @@
     def _(c):
         part = packed.at[pl.ds(0, n_stn * INNER - 1), c]
         pltpu.make_async_copy(part, part, send1.at[c]).wait()
-        for block in range(n_out):
-            @pl.when(jnp.logical_and(has_right, outer >= block))
-            def _():
-                line(c, block, 1).wait_send()
-
-            @pl.when(jnp.logical_and(has_left, outer <= block))
-            def _():
-                line(c, block, 0).wait_send()
+
+        @pl.when(c >= count - WINDOW)
+        def _():
+            for block in range(n_out):
+                @pl.when(jnp.logical_and(has_right, outer >= block))
+                def _():
+                    line(c, block, 1).wait_send()
+
+                @pl.when(jnp.logical_and(has_left, outer <= block))
+                def _():
+                    line(c, block, 0).wait_send()
 
         back(c).wait_send()
         back(c).wait_recv()

time: 180 us -> 177 us (0.983)
  Pallas kernels: 177 us -> 174 us
    pallas_call x1, Pallas kernels: 168 us -> 166 us  [gather_and_correlate(): pl.pallas_call(functools.partial(gather_kernel, n_stn, n_out), out_shape=...]
where the time goes in v3:
time: 177 us
  Pallas kernels  174 us (98%)
  local copies, waits for them, and re-layouts  2.05 us (1%)
    pallas_call x1, Pallas kernels, gather_and_correlate(): pl.pallas_call(functools.partial(gather_kernel, n_stn, n_out), out_shape=...  166 us
    pallas_call x1, Pallas kernels, spread(): pl.pallas_call(spread_kernel, out_shape=jax.ShapeDtypeStruct((group_size,...  8.74 us

profile of v3, /device:TPU:0, one launch (start us, length us, event | category | flops | bytes accessed | tf_op | source)
XLA Modules:
  0.0 177.1 jit_solution(9788779475865313150)
XLA Ops:
  0.6 0.8 copy.7
  1.4 0.1 copy.8
  1.5 0.6 reshape.11.plan
  2.2 165.6 %shard_map.50 = (bf16[16,2,128,1024]{3,2,1,0:T(8,128)(2,1)}, f32[1,1,2]{2,1,0:T(1,128)}) custom-call(s32[64]{0:T(128)} %reshape.11.plan, bf16[2,96,32,256]{3,2,1,0:T(8,128)(2,1)} %voltages.1), custom_call_target="tpu_custom_call" | custom-call | tf_op jit(solution)/shard_map/pallas_call | solution.py:178
  167.8 0.0 copy-start
  167.8 8.7 %shard_map.51 = bf16[24,2,128,1024]{3,2,1,0:T(8,128)(2,1)} custom-call(s32[64]{0:T(128)} %reshape.11.plan, s32[32]{0:T(128)} %flagged.1, bf16[16,2,128,1024]{3,2,1,0:T(8,128)(2,1)} %get-tuple-element.4.made), custom_call_target="tpu_custom_call" | custom-call | tf_op jit(solution)/shard_map/pallas_call | solution.py:231
  176.5 0.0 copy-done
  176.5 0.5 copy.10
Async XLA Ops:
  167.8 8.8 %copy-start = (f32[1,1,2]{2,1,0:T(1,128)S(1)}, f32[1,1,2]{2,1,0:T(1,128)}, u32[]{:S(2)}) copy-start(f32[1,1,2]{2,1,0:T(1,128)} %get-tuple-element.9) | copy-start | bytes 28

commit v4 on v3

--- a/solution.py
+++ b/solution.py
@@ -178,7 +178,7 @@
     return pl.pallas_call(
         functools.partial(gather_kernel, n_stn, n_out),
         out_shape=(
-            jax.ShapeDtypeStruct((INNER * count, 2, rows, total_rows), jnp.bfloat16),
+            pltpu.VMEM((INNER * count, 2, rows, total_rows), jnp.bfloat16),
             jax.ShapeDtypeStruct((1, 1, count // n_out), jnp.float32),
         ),
         in_specs=[pl.BlockSpec(memory_space=pltpu.SMEM), pl.BlockSpec(memory_space=pltpu.VMEM)],
@@ -192,34 +192,28 @@
             dma((count,)), dma((count,)), dma((count,)),
         ],
         compiler_params=pltpu.CompilerParams(
-            collective_id=0, has_side_effects=True, vmem_limit_bytes=56 * 1024 * 1024
+            collective_id=0, has_side_effects=True, vmem_limit_bytes=30 * 1024 * 1024
         ),
     )(plan, voltages)
 
 
-def spread_kernel(plan, flagged, made, out, zeros, held, read_sem, write_sem, zero_sem):
+def spread_kernel(plan, flagged, made, out, zeros, write_sem, zero_sem):
     stn = lax.axis_index("stn")
     slots, group_size = made.shape[0], out.shape[0]
     first = stn * group_size
     idle = group_size - slots
 
-    def read(j):
-        return pltpu.make_async_copy(made.at[j], held.at[j], read_sem.at[j])
-
     def write(j):
-        return pltpu.make_async_copy(held.at[j], out.at[plan[stn * slots + j] - first], write_sem.at[j])
+        return pltpu.make_async_copy(made.at[j], out.at[plan[stn * slots + j] - first], write_sem.at[j])
 
     def clear(j):
         return pltpu.make_async_copy(zeros, out.at[flagged[stn * idle + j] - first], zero_sem.at[j])
 
     for j in range(slots):
-        read(j).start()
+        write(j).start()
     zeros[...] = jnp.zeros_like(zeros)
     for j in range(idle):
         clear(j).start()
-    for j in range(slots):
-        read(j).wait()
-        write(j).start()
     for j in range(slots):
         write(j).wait()
     for j in range(idle):
@@ -235,12 +229,10 @@
         out_specs=pl.BlockSpec(memory_space=pl.ANY),
         scratch_shapes=[
             pltpu.VMEM(made.shape[1:], made.dtype),
-            pltpu.VMEM(made.shape, made.dtype),
-            pltpu.SemaphoreType.DMA((slots,)),
             pltpu.SemaphoreType.DMA((slots,)),
             pltpu.SemaphoreType.DMA((idle,)),
         ],
-        compiler_params=pltpu.CompilerParams(vmem_limit_bytes=56 * 1024 * 1024),
+        compiler_params=pltpu.CompilerParams(vmem_limit_bytes=16 * 1024 * 1024),
     )(plan, flagged, made)
 
 

time: 177 us -> 174 us (0.983)
  Pallas kernels: 174 us -> 169 us
  local copies, waits for them, and re-layouts: 2.05 us -> 4.07 us
    pallas_call x1, Pallas kernels: 8.74 us -> 5.3 us  [spread(): pl.pallas_call(spread_kernel, out_shape=jax.ShapeDtypeStruct((group_size,...]
    unnamed x4 -> x6, local copies, waits for them, and re-layouts: 1.29 us -> 3.82 us
where the time goes in v4:
time: 174 us
  Pallas kernels  169 us (97%)
  local copies, waits for them, and re-layouts  4.07 us (2%)
    pallas_call x1, Pallas kernels, gather_and_correlate(): pl.pallas_call(functools.partial(gather_kernel, n_stn, n_out), out_shape=...  164 us
    pallas_call x1, Pallas kernels, spread(): pl.pallas_call(spread_kernel, out_shape=jax.ShapeDtypeStruct((group_size,...  5.3 us
    unnamed x6, local copies, waits for them, and re-layouts  3.82 us

profile of v4, /device:TPU:0, one launch (start us, length us, event | category | flops | bytes accessed | tf_op | source)
XLA Modules:
  0.0 174.1 jit_solution(6042266625890576586)
XLA Ops:
  0.6 0.8 copy.7
  1.4 0.1 copy.8
  1.5 0.1 reshape.11.plan
  1.6 0.0 copy-start
  1.7 1.9 %copy-done = bf16[2,96,32,256]{3,2,1,0:T(8,128)(2,1)S(1)} copy-done((bf16[2,96,32,256]{3,2,1,0:T(8,128)(2,1)S(1)}, bf16[2,96,32,256]{3,2,1,0:T(8,128)(2,1)}, u32[]{:S(2)}) %copy-start) | copy-done | bytes 3145752
  3.5 164.1 %shard_map.50 = (bf16[16,2,128,1024]{3,2,1,0:T(8,128)(2,1)S(1)}, f32[1,1,2]{2,1,0:T(1,128)S(1)}) custom-call(s32[64]{0:T(128)S(1)} %reshape.11.plan, bf16[2,96,32,256]{3,2,1,0:T(8,128)(2,1)S(1)} %copy-done), custom_call_target="tpu_custom_call" | custom-call | tf_op jit(solution)/shard_map/pallas_call | solution.py:178
  167.7 0.0 copy-start.1
  167.7 0.6 copy-done.1
  168.3 5.3 %shard_map.51 = bf16[24,2,128,1024]{3,2,1,0:T(8,128)(2,1)} custom-call(s32[64]{0:T(128)S(1)} %reshape.11.plan, s32[32]{0:T(128)S(1)} %copy-done.1, bf16[16,2,128,1024]{3,2,1,0:T(8,128)(2,1)S(1)} %get-tuple-element.4.made), custom_call_target="tpu_custom_call" | custom-call | tf_op jit(solution)/shard_map/pallas_call | solution.py:225
  173.6 0.5 copy.10
Async XLA Ops:
  1.6 1.9 %copy-start = (bf16[2,96,32,256]{3,2,1,0:T(8,128)(2,1)S(1)}, bf16[2,96,32,256]{3,2,1,0:T(8,128)(2,1)}, u32[]{:S(2)}) copy-start(bf16[2,96,32,256]{3,2,1,0:T(8,128)(2,1)} %voltages.1) | copy-start | bytes 9437188
  167.7 0.7 copy-start.1

commit v5 on v4

--- a/solution.py
+++ b/solution.py
@@ -14,13 +14,14 @@
 INNER = 2
 
 
-def gather_kernel(n_stn, n_out, plan, voltages, own_out, power, packed, full, made, recv1, send1, recv2, send2, send3, recv3, local3):
+def gather_kernel(n_stn, n_out, plan, voltages, own_out, power, packed, full, extra, made, recv1, send1, recv2, send2, send3, recv3, local3, send4, recv4):
     stn = lax.axis_index("stn")
     chan = lax.axis_index("chan")
     outer, inner = chan // INNER, chan % INNER
     count, stations = packed.shape[1], packed.shape[2]
     time = voltages.shape[3]
     scale = 1.0 / time
+    last = count - 1
     has_left, has_right = outer > 0, outer < n_out - 1
 
     barrier = pltpu.get_barrier_semaphore()
@@ -75,17 +76,23 @@
             device_id=(stn, outer * INNER + 1 - inner), device_id_type=MESH,
         )
 
-    def keep(c):
-        return pltpu.make_async_copy(made.at[c, inner], own_out.at[inner * count + c], local3.at[c])
-
-    def correlate(c, half):
+    def keep(c, half, sem):
+        return pltpu.make_async_copy(made.at[c, half], own_out.at[half * count + c], local3.at[sem])
+
+    def share(block):
+        return pltpu.make_async_remote_copy(
+            full.at[last, :, block], extra.at[:, block], send4.at[block], recv4.at[block],
+            device_id=(stn, outer * INNER + 1 - inner), device_id_type=MESH,
+        )
+
+    def correlate(source, c, rows_of, half):
         span = INNER * stations
         pieces = n_out // INNER
-        left = full[c, outer, pl.ds(half * pieces, pieces)].reshape(pieces * span, -1)
+        left = source[outer, pl.ds(rows_of * pieces, pieces)].reshape(pieces * span, -1)
         turned = jnp.concatenate([left[:, time:], -left[:, :time]], axis=1)
         both = jnp.concatenate([left, turned], axis=0)
         for col in range(n_stn):
-            right = full[c, col].reshape(n_out * span, -1)
+            right = source[col].reshape(n_out * span, -1)
             product = lax.dot_general(both, right, (((1,), (1,)), ((), ())), preferred_element_type=jnp.float32)
             made[c, half, :, :, col * n_out * span:(col + 1) * n_out * span] = (
                 (product * scale).astype(jnp.bfloat16).reshape(2, pieces * span, n_out * span)
@@ -113,6 +120,10 @@
             def _():
                 send(t, outer, 1)
 
+            @pl.when(t == last)
+            def _():
+                share(outer).start()
+
         c = t - LEAD
         live = c >= 0
         for d in range(1, n_out):
@@ -125,6 +136,10 @@
                 def _():
                     send(c, outer - d, 1)
 
+                @pl.when(c == last)
+                def _():
+                    share(outer - d).start()
+
             @pl.when(jnp.logical_and(live, outer + d < n_out))
             def _():
                 line(c, outer + d, 0).wait_recv()
@@ -133,12 +148,19 @@
                 def _():
                     send(c, outer + d, 0)
 
+                @pl.when(c == last)
+                def _():
+                    share(outer + d).start()
+
         @pl.when(live)
         def _():
-            correlate(c, 1 - inner)
-            back(c).start()
-            correlate(c, inner)
-            keep(c).start()
+            @pl.when(c < last)
+            def _():
+                correlate(full.at[c], c, 1 - inner, 1 - inner)
+                back(c).start()
+
+            correlate(full.at[c], c, inner, inner)
+            keep(c, inner, c).start()
 
     for k in range(count // n_out):
         total = jnp.zeros((8, full.shape[4]), jnp.float32)
@@ -147,6 +169,11 @@
             total = total + jnp.sum((values * values).reshape(-1, 8, full.shape[4]), axis=0)
         power[0, 0, k] = jnp.sum(total) * scale / (n_stn * n_out * INNER * stations)
 
+    for block in range(n_out):
+        share(block).wait_recv()
+    correlate(extra, last, inner, 1 - inner)
+    keep(last, 1 - inner, count).start()
+
     @pl.loop(0, count)
     def _(c):
         part = packed.at[pl.ds(0, n_stn * INNER - 1), c]
@@ -163,9 +190,16 @@
                 def _():
                     line(c, block, 0).wait_send()
 
-        back(c).wait_send()
-        back(c).wait_recv()
-        keep(c).wait()
+        @pl.when(c < last)
+        def _():
+            back(c).wait_send()
+            back(c).wait_recv()
+
+        keep(c, inner, c).wait()
+
+    keep(last, 1 - inner, count).wait()
+    for block in range(n_out):
+        share(block).wait_send()
 
 
 def gather_and_correlate(plan, voltages, n_stn, n_out):
@@ -186,10 +220,12 @@
         scratch_shapes=[
             pltpu.VMEM((n_stn * INNER, count, stations, depth), jnp.bfloat16),
             pltpu.VMEM((count, n_stn, n_out, INNER * stations, depth), jnp.bfloat16),
+            pltpu.VMEM((n_stn, n_out, INNER * stations, depth), jnp.bfloat16),
             pltpu.VMEM((count, INNER, 2, rows, total_rows), jnp.bfloat16),
             dma((count,)), dma((count,)),
             dma((n_out, count)), dma((2, n_out, count)),
-            dma((count,)), dma((count,)), dma((count,)),
+            dma((count,)), dma((count,)), dma((count + 1,)),
+            dma((n_out,)), dma((n_out,)),
         ],
         compiler_params=pltpu.CompilerParams(
             collective_id=0, has_side_effects=True, vmem_limit_bytes=30 * 1024 * 1024

time: 174 us -> 181 us (1.040)
  Pallas kernels: 169 us -> 176 us
    pallas_call x1, Pallas kernels: 164 us -> 171 us  [gather_and_correlate(): pl.pallas_call(functools.partial(gather_kernel, n_stn, n_out), out_shape=...]
where the time goes in v5:
time: 181 us
  Pallas kernels  176 us (97%)
  local copies, waits for them, and re-layouts  4.07 us (2%)
    pallas_call x1, Pallas kernels, gather_and_correlate(): pl.pallas_call(functools.partial(gather_kernel, n_stn, n_out), out_shape=...  171 us
    pallas_call x1, Pallas kernels, spread(): pl.pallas_call(spread_kernel, out_shape=jax.ShapeDtypeStruct((group_size,...  5.3 us
    unnamed x6, local copies, waits for them, and re-layouts  3.82 us

profile of v5, /device:TPU:0, one launch (start us, length us, event | category | flops | bytes accessed | tf_op | source)
XLA Modules:
  0.0 180.6 jit_solution(16263092274660278869)
XLA Ops:
  0.6 0.8 copy.7
  1.4 0.1 copy.8
  1.5 0.1 reshape.11.plan
  1.6 0.0 copy-start
  1.7 1.9 %copy-done = bf16[2,96,32,256]{3,2,1,0:T(8,128)(2,1)S(1)} copy-done((bf16[2,96,32,256]{3,2,1,0:T(8,128)(2,1)S(1)}, bf16[2,96,32,256]{3,2,1,0:T(8,128)(2,1)}, u32[]{:S(2)}) %copy-start) | copy-done | bytes 3145752
  3.5 170.6 %shard_map.50 = (bf16[16,2,128,1024]{3,2,1,0:T(8,128)(2,1)S(1)}, f32[1,1,2]{2,1,0:T(1,128)S(1)}) custom-call(s32[64]{0:T(128)S(1)} %reshape.11.plan, bf16[2,96,32,256]{3,2,1,0:T(8,128)(2,1)S(1)} %copy-done), custom_call_target="tpu_custom_call" | custom-call | tf_op jit(solution)/shard_map/pallas_call | solution.py:212
  174.1 0.0 copy-start.1
  174.1 0.6 copy-done.1
  174.8 5.3 %shard_map.51 = bf16[24,2,128,1024]{3,2,1,0:T(8,128)(2,1)} custom-call(s32[64]{0:T(128)S(1)} %reshape.11.plan, s32[32]{0:T(128)S(1)} %copy-done.1, bf16[16,2,128,1024]{3,2,1,0:T(8,128)(2,1)S(1)} %get-tuple-element.4.made), custom_call_target="tpu_custom_call" | custom-call | tf_op jit(solution)/shard_map/pallas_call | solution.py:261
  180.1 0.5 copy.10
Async XLA Ops:
  1.6 1.9 %copy-start = (bf16[2,96,32,256]{3,2,1,0:T(8,128)(2,1)S(1)}, bf16[2,96,32,256]{3,2,1,0:T(8,128)(2,1)}, u32[]{:S(2)}) copy-start(bf16[2,96,32,256]{3,2,1,0:T(8,128)(2,1)} %voltages.1) | copy-start | bytes 9437188
  174.1 0.7 copy-start.1

commit v6 on v4

--- a/solution.py
+++ b/solution.py
@@ -20,6 +20,7 @@
     outer, inner = chan // INNER, chan % INNER
     count, stations = packed.shape[1], packed.shape[2]
     time = voltages.shape[3]
+    slots = plan.shape[2]
     scale = 1.0 / time
     has_left, has_right = outer > 0, outer < n_out - 1
 
@@ -43,7 +44,7 @@
 
     def turn(c):
         for dest in range(n_stn * INNER):
-            channel = plan[dest * count + c]
+            channel = plan[dest // INNER, (c // slots) * INNER + dest % INNER, c % slots]
             for part in range(2):
                 packed[dest, c, :, part * time:(part + 1) * time] = voltages[part, channel]
         rows = pl.ds(pl.multiple_of(inner * stations, stations), stations)
@@ -170,7 +171,7 @@
 
 def gather_and_correlate(plan, voltages, n_stn, n_out):
     _, _, stations, time = voltages.shape
-    count = plan.shape[0] // (n_stn * INNER)
+    count = n_out * plan.shape[2]
     depth = 2 * time
     total_rows = n_stn * n_out * INNER * stations
     rows = total_rows // (n_out * INNER)
@@ -192,7 +193,7 @@
             dma((count,)), dma((count,)), dma((count,)),
         ],
         compiler_params=pltpu.CompilerParams(
-            collective_id=0, has_side_effects=True, vmem_limit_bytes=30 * 1024 * 1024
+            collective_id=0, has_side_effects=True, vmem_limit_bytes=54 * 1024 * 1024
         ),
     )(plan, voltages)
 
@@ -203,8 +204,12 @@
     first = stn * group_size
     idle = group_size - slots
 
+    depth = plan.shape[2]
+    count = slots // INNER
+
     def write(j):
-        return pltpu.make_async_copy(made.at[j], out.at[plan[stn * slots + j] - first], write_sem.at[j])
+        channel = plan[stn, (j % count) // depth * INNER + j // count, j % depth]
+        return pltpu.make_async_copy(made.at[j], out.at[channel - first], write_sem.at[j])
 
     def clear(j):
         return pltpu.make_async_copy(zeros, out.at[flagged[stn * idle + j] - first], zero_sem.at[j])
@@ -264,12 +269,12 @@
     n_out = n_chan // INNER
     _, channels, stations, _ = voltages.shape
     slot_count = work_plan.shape[2]
-    plan = work_plan.reshape(n_stn, n_out, INNER, slot_count).transpose(0, 2, 1, 3).reshape(-1)
     if n_stn == n_out and stations % 16 == 0:
-        made, power = gather_and_correlate(plan, voltages, n_stn, n_out)
+        made, power = gather_and_correlate(work_plan, voltages, n_stn, n_out)
     else:
+        plan = work_plan.reshape(n_stn, n_out, INNER, slot_count).transpose(0, 2, 1, 3).reshape(-1)
         made, power = correlate_gathered(plan, voltages, n_stn, n_out)
-    return spread(plan, flagged_ids, made, channels // n_stn), power
+    return spread(work_plan, flagged_ids, made, channels // n_stn), power
 
 
 def solution(mesh):

time: 174 us -> 175 us (level)
  Pallas kernels: 169 us -> 171 us
    unnamed x6 -> x8, local copies, waits for them, and re-layouts: 3.82 us -> 3.27 us
where the time goes in v6:
time: 175 us
  Pallas kernels  171 us (98%)
  local copies, waits for them, and re-layouts  3.27 us (2%)
    pallas_call x1, Pallas kernels, gather_and_correlate(): pl.pallas_call(functools.partial(gather_kernel, n_stn, n_out), out_shape=...  165 us
    pallas_call x1, Pallas kernels, spread(): pl.pallas_call(spread_kernel, out_shape=jax.ShapeDtypeStruct((group_size,...  5.56 us

profile of v6, /device:TPU:0, one launch (start us, length us, event | category | flops | bytes accessed | tf_op | source)
XLA Modules:
  0.0 174.9 jit_solution(7041579224303543390)
XLA Ops:
  0.6 1.4 copy.6.plan
  2.0 165.4 %shard_map.50 = (bf16[16,2,128,1024]{3,2,1,0:T(8,128)(2,1)S(1)}, f32[1,1,2]{2,1,0:T(1,128)}) custom-call(s32[4,8,2]{2,1,0:T(8,128)} %copy.6.plan, bf16[2,96,32,256]{3,2,1,0:T(8,128)(2,1)} %voltages.1), custom_call_target="tpu_custom_call" | custom-call | tf_op jit(solution)/shard_map/pallas_call | solution.py:179
  167.4 0.0 copy-start
  167.4 0.7 copy-done
  168.1 0.0 copy-start.1
  168.1 0.7 copy-done.1
  168.8 0.0 copy-start.2
  168.8 5.6 %shard_map.51 = bf16[24,2,128,1024]{3,2,1,0:T(8,128)(2,1)} custom-call(s32[4,8,2]{2,1,0:T(8,128)S(1)} %copy-done, s32[32]{0:T(128)S(1)} %copy-done.1, bf16[16,2,128,1024]{3,2,1,0:T(8,128)(2,1)S(1)} %get-tuple-element.4.made), custom_call_target="tpu_custom_call" | custom-call | tf_op jit(solution)/shard_map/pallas_call | solution.py:230
  174.4 0.0 copy-done.2
  174.4 0.5 copy.8
Async XLA Ops:
  167.4 0.7 copy-start
  168.1 0.7 copy-start.1
  168.8 5.6 %copy-start.2 = (f32[1,1,2]{2,1,0:T(1,128)S(1)}, f32[1,1,2]{2,1,0:T(1,128)}, u32[]{:S(2)}) copy-start(f32[1,1,2]{2,1,0:T(1,128)} %get-tuple-element.9) | copy-start | bytes 28

commit v7 on v6

--- a/solution.py
+++ b/solution.py
@@ -193,7 +193,7 @@
             dma((count,)), dma((count,)), dma((count,)),
         ],
         compiler_params=pltpu.CompilerParams(
-            collective_id=0, has_side_effects=True, vmem_limit_bytes=54 * 1024 * 1024
+            collective_id=0, has_side_effects=True, vmem_limit_bytes=30 * 1024 * 1024
         ),
     )(plan, voltages)
 

time: 175 us -> 175 us (level)
    unnamed x8 -> x6, local copies, waits for them, and re-layouts: 3.27 us -> 3.83 us
where the time goes in v7:
time: 175 us; the launch traced here: 174 us
  Pallas kernels  170 us (97%)
  local copies, waits for them, and re-layouts  3.83 us (2%)
    pallas_call x1, Pallas kernels, gather_and_correlate(): pl.pallas_call(functools.partial(gather_kernel, n_stn, n_out), out_shape=...  164 us
    pallas_call x1, Pallas kernels, spread(): pl.pallas_call(spread_kernel, out_shape=jax.ShapeDtypeStruct((group_size,...  5.56 us
    unnamed x6, local copies, waits for them, and re-layouts  3.83 us

profile of v7, /device:TPU:0, one launch (start us, length us, event | category | flops | bytes accessed | tf_op | source)
XLA Modules:
  0.0 174.4 jit_solution(12438154646361811679)
XLA Ops:
  0.6 0.8 copy.6.plan
  1.4 0.0 copy-start
  1.4 1.9 %copy-done = bf16[2,96,32,256]{3,2,1,0:T(8,128)(2,1)S(1)} copy-done((bf16[2,96,32,256]{3,2,1,0:T(8,128)(2,1)S(1)}, bf16[2,96,32,256]{3,2,1,0:T(8,128)(2,1)}, u32[]{:S(2)}) %copy-start) | copy-done | bytes 3145752
  3.3 164.4 %shard_map.50 = (bf16[16,2,128,1024]{3,2,1,0:T(8,128)(2,1)S(1)}, f32[1,1,2]{2,1,0:T(1,128)S(1)}) custom-call(s32[4,8,2]{2,1,0:T(8,128)S(1)} %copy.6.plan, bf16[2,96,32,256]{3,2,1,0:T(8,128)(2,1)S(1)} %copy-done), custom_call_target="tpu_custom_call" | custom-call | tf_op jit(solution)/shard_map/pallas_call | solution.py:179
  167.7 0.0 copy-start.1
  167.7 0.6 copy-done.1
  168.3 5.6 %shard_map.51 = bf16[24,2,128,1024]{3,2,1,0:T(8,128)(2,1)} custom-call(s32[4,8,2]{2,1,0:T(8,128)S(1)} %copy.6.plan, s32[32]{0:T(128)S(1)} %copy-done.1, bf16[16,2,128,1024]{3,2,1,0:T(8,128)(2,1)S(1)} %get-tuple-element.4.made), custom_call_target="tpu_custom_call" | custom-call | tf_op jit(solution)/shard_map/pallas_call | solution.py:230
  173.9 0.5 copy.8
Async XLA Ops:
  1.4 1.9 %copy-start = (bf16[2,96,32,256]{3,2,1,0:T(8,128)(2,1)S(1)}, bf16[2,96,32,256]{3,2,1,0:T(8,128)(2,1)}, u32[]{:S(2)}) copy-start(bf16[2,96,32,256]{3,2,1,0:T(8,128)(2,1)} %voltages.1) | copy-start | bytes 9437188
  167.7 0.7 copy-start.1
